TPU v7x, 32 devices: a whole 2x2x4 slice. The times are simulated.
32 devices in a mesh: grp: 2 (over y), gy: 4 (over z), gx: 2 (over x), ch: 2 (over core).
Axes of the slice: x: 2, y: 2, z: 4, core: 2. Of those that a mesh axis runs over, the one named last changes fastest.
Arguments:
- cells: bfloat16 [128, 128, 512], P(('grp', 'gy'), 'gx'), parts along dimension 0, may hold values from -6 to 6
- w_expand: bfloat16 [512, 2048], P(None, 'ch'), may hold values from -0.25 to 0.25
- b_expand: float32 [2048], P('ch'), may hold values from -3 to 3
- w_depth: bfloat16 [3, 3, 2048], P(None, None, 'ch'), may hold values from -2 to 2
- b_depth: float32 [2048], P('ch'), may hold values from -3 to 3
- w_project: bfloat16 [2048, 512], P('ch'), may hold values from -0.125 to 0.125
- b_project: float32 [512], replicated, may hold values from -3 to 3
- ln_gain: float32 [512], replicated, may hold values from 0.5 to 1.5
- w_qkv: bfloat16 [512, 3, 512], P(None, None, 'ch'), as said below
- w_out: bfloat16 [512, 512], P('ch'), may hold values from -0.25 to 0.25
- b_out: float32 [512], P('ch'), may hold values from -3 to 3
Outputs:
- result: bfloat16 [128, 128, 512], P(('grp', 'gy'), 'gx', 'ch'), parts along dimension 0
There are 2 independent parts, one for each index of `grp`. A program takes and returns all parts, laid end to end along the dimension named above; an argument that names none is the same for every part. Nothing has to cross between parts.
Inputs may be any that keep to these rules, and one draw needn't show every extreme that they name: `w_qkv`: dense projection weights of every head.
All inputs are finite; a program needn't handle non-finite values.
Results may differ from a plain program's by a relative error of at most 0.01.
Values may be sent and summed in bfloat16 or wider, within the bound.
A program may use at most 64 MiB of HBM per device.

v0:
```python
import jax
import jax.numpy as jnp
from jax import lax
from jax.sharding import PartitionSpec as P

HEAD_DIM = 32
GRID = 8


def extended(block, sides, width):
    for axis, dim in sides:
        count = lax.axis_size(axis)
        forward = [(i, i + 1) for i in range(count - 1)]
        backward = [(target, source) for source, target in forward]
        low = lax.ppermute(
            lax.slice_in_dim(block, block.shape[dim] - width, None, axis=dim), axis, forward
        )
        high = lax.ppermute(lax.slice_in_dim(block, 0, width, axis=dim), axis, backward)
        block = jnp.concatenate([low, block, high], axis=dim)
    return block


def gelu_exact(values):
    return jax.nn.gelu(values, approximate=False)


def expand_cells(source, w_expand, b_expand):
    pre = jnp.einsum("hwc,ce->hwe", source, w_expand, preferred_element_type=jnp.float32)
    return gelu_exact(pre + b_expand).astype(jnp.bfloat16)


def depthwise(padded, w_depth, b_depth, tile_h, tile_w):
    summed = jnp.zeros((tile_h, tile_w, padded.shape[2]), jnp.float32)
    for row_off in range(3):
        for col_off in range(3):
            summed = summed + padded[row_off : row_off + tile_h, col_off : col_off + tile_w].astype(
                jnp.float32
            ) * w_depth[row_off, col_off].astype(jnp.float32)
    return gelu_exact(summed + b_depth).astype(jnp.bfloat16)


def split_order(tile, depth_h, depth_w):
    tile_h, tile_w, width = tile.shape
    shaped = tile.reshape(tile_h // depth_h, depth_h, tile_w // depth_w, depth_w, width)
    return shaped.transpose(1, 0, 3, 2, 4)


def join_order(arranged):
    depth_h, outer_h, depth_w, outer_w, width = arranged.shape
    return arranged.transpose(1, 0, 3, 2, 4).reshape(outer_h * depth_h, outer_w * depth_w, width)


def into_windows(arrived, steps_h, steps_w):
    local_h, span_h, local_w, span_w, width = arrived.shape
    grouped = arrived.reshape(local_h, GRID, steps_h, local_w, GRID, steps_w, width)
    grouped = grouped.transpose(2, 0, 5, 3, 1, 4, 6)
    return grouped.reshape(steps_h * local_h * steps_w * local_w, GRID * GRID, width)


def out_of_windows(windows, local_h, steps_h, local_w, steps_w):
    width = windows.shape[2]
    grouped = windows.reshape(steps_h, local_h, steps_w, local_w, GRID, GRID, width)
    grouped = grouped.transpose(1, 4, 0, 3, 5, 2, 6)
    return grouped.reshape(local_h, GRID * steps_h, local_w, GRID * steps_w, width)


def attend(window_full, ln_gain, w_qkv):
    values = window_full.astype(jnp.float32)
    centre = jnp.mean(values, axis=-1, keepdims=True)
    centered = values - centre
    spread = jnp.mean(centered * centered, axis=-1, keepdims=True)
    normed = (centered * lax.rsqrt(spread + 1e-05) * ln_gain).astype(jnp.bfloat16)
    projected = jnp.einsum(
        "wtc,cke->kwte", normed, w_qkv, preferred_element_type=jnp.float32
    ).astype(jnp.bfloat16)
    window_count = projected.shape[1]
    tokens = projected.shape[2]
    own_width = projected.shape[3]
    heads_own = own_width // HEAD_DIM
    shaped = projected.reshape(3, window_count, tokens, heads_own, HEAD_DIM)
    scores = jnp.einsum(
        "wqhd,wkhd->whqk", shaped[0], shaped[1], preferred_element_type=jnp.float32
    ) * HEAD_DIM ** (-0.5)
    weights = jax.nn.softmax(scores, axis=-1).astype(jnp.bfloat16)
    heads_out = jnp.einsum(
        "whqk,wkhd->wqhd", weights, shaped[2], preferred_element_type=jnp.float32
    ).astype(jnp.bfloat16)
    return heads_out.reshape(window_count, tokens, own_width)


def per_device(
    cells, w_expand, b_expand, w_depth, b_depth, w_project, b_project, ln_gain, w_qkv, w_out, b_out
):
    tile_h, tile_w, width = cells.shape
    n_rows = lax.axis_size("gy")
    n_cols = lax.axis_size("gx")
    half = width // lax.axis_size("ch")
    own = lax.axis_index("ch")
    stride_h = tile_h * n_rows // GRID
    stride_w = tile_w * n_cols // GRID
    depth_h = min(tile_h, stride_h)
    depth_w = min(tile_w, stride_w)
    steps_h = stride_h // depth_h
    steps_w = stride_w // depth_w
    local_h = depth_h // n_rows
    local_w = depth_w // n_cols
    expanded = expand_cells(cells, w_expand, b_expand)
    padded = extended(expanded, (("gy", 0), ("gx", 1)), 1)
    depth = depthwise(padded, w_depth, b_depth, tile_h, tile_w)
    partial_value = jnp.einsum("hwe,ec->hwc", depth, w_project, preferred_element_type=jnp.float32)
    share = lax.psum_scatter(
        partial_value.astype(jnp.bfloat16), "ch", scatter_dimension=2, tiled=True
    ).astype(jnp.float32)
    cells_own = lax.dynamic_slice_in_dim(cells, own * half, half, 2)
    bias_own = lax.dynamic_slice_in_dim(b_project, own * half, half, 0)
    mixed_own = (cells_own.astype(jnp.float32) + share + bias_own).astype(jnp.bfloat16)
    arranged = split_order(mixed_own, depth_h, depth_w)
    arrived = lax.all_to_all(
        lax.all_to_all(arranged, "gy", split_axis=0, concat_axis=1, tiled=True),
        "gx",
        split_axis=2,
        concat_axis=3,
        tiled=True,
    )
    window_own = into_windows(arrived, steps_h, steps_w)
    window_full = lax.all_gather(window_own, "ch", axis=2, tiled=True)
    heads_out = attend(window_full, ln_gain, w_qkv)
    attention_terms = jnp.einsum(
        "wte,ec->wtc", heads_out, w_out, preferred_element_type=jnp.float32
    )
    attention_own = lax.psum_scatter(
        attention_terms.astype(jnp.bfloat16), "ch", scatter_dimension=2, tiled=True
    ).astype(jnp.float32)
    outcome = (window_own.astype(jnp.float32) + attention_own + b_out).astype(jnp.bfloat16)
    leaving = out_of_windows(outcome, local_h, steps_h, local_w, steps_w)
    returned = lax.all_to_all(
        lax.all_to_all(leaving, "gy", split_axis=1, concat_axis=0, tiled=True),
        "gx",
        split_axis=3,
        concat_axis=2,
        tiled=True,
    )
    return join_order(returned)


def solution(mesh):
    placed = (
        P(("grp", "gy"), "gx", None),
        P(None, "ch"),
        P("ch"),
        P(None, None, "ch"),
        P("ch"),
        P("ch", None),
        P(),
        P(),
        P(None, None, "ch"),
        P("ch", None),
        P("ch"),
    )
    return jax.shard_map(
        per_device,
        mesh=mesh,
        in_specs=placed,
        out_specs=P(("grp", "gy"), "gx", "ch"),
        check_vma=False,
    )
```

profile of v0, /device:TPU:0, one launch (start us, length us, event | category | flops | bytes accessed | tf_op | source)
XLA Modules:
  0.0 172.8 jit_solution(14447572569704020268)
XLA Ops:
  6.5 1.2 copy-done
  7.8 11.1 %fusion.3 = bf16[16,64,1024]{2,1,0:T(8,128)(2,1)S(1)} fusion(bf16[16,64,512]{2,1,0:T(8,128)(2,1)} %param.11, f32[1024]{0:T(1024)} %param.13, bf16[512,1024]{1,0:T(8,128)(2,1)S(1)} %copy-done), kind=kOutput, calls=%fused_computation.5 | convolution fusion | flops 1142947840 | bytes 4198400 | tf_op jit(solution)/shard_map/hwc,ce->hwe/dot_general | solution.py:28
  18.9 5.0 %collective-permute-start = (bf16[1,64,1024]{2,1,0:T(8,128)(2,1)S(1)}, bf16[1,64,1024]{2,1,0:T(8,128)(2,1)S(1)}, u32[]{:S(2)}, u32[]{:S(2)}) collective-permute-start(bf16[1,64,1024]{2,1,0:T(8,128)(2,1)S(1)} %get-tuple-element.9), channel_id=1, source_target_pairs={{0,4},{4,8},{8,12},{1,5},{5,9},{9,13},{2,6},{6,10},{10,14},{3,7},{... | collective-permute-start | bytes 393224 | tf_op jit(solution)/shard_map/ppermute | solution.py:15
  23.8 1.3 collective-permute-start.1
  25.1 1.4 collective-permute-done
  26.6 4.1 %collective-permute-done.1 = bf16[1,64,1024]{2,1,0:T(8,128)(2,1)S(1)} collective-permute-done((bf16[1,64,1024]{2,1,0:T(8,128)(2,1)S(1)}, bf16[1,64,1024]{2,1,0:T(8,128)(2,1)S(1)}, u32[]{:S(2)}, u32[]{:S(2)}) %collective-permute-start.1) | collective-permute-done | bytes 131104 | tf_op jit(solution)/shard_map/ppermute | solution.py:18
  30.7 0.1 pad_maximum_fusion.5
  30.8 0.0 copy-start.7
  30.8 0.0 copy-start.9
  30.8 3.5 %collective-permute-start.2 = (bf16[18,1,1024]{2,1,0:T(2,128)(2,1)S(1)}, bf16[18,1,1024]{2,1,0:T(2,128)(2,1)S(1)}, u32[]{:S(2)}, u32[]{:S(2)}) collective-permute-start(bf16[18,1,1024]{2,1,0:T(2,128)(2,1)S(1)} %get-tuple-element.7), channel_id=1, source_target_pairs={{0,2},{1,3},{4,6},{5,7},{8,10},{9,11},{12,14},{13,15},{16,18},{17,... | collective-permute-start | bytes 110600 | tf_op jit(solution)/shard_map/ppermute | solution.py:15
  34.4 1.3 collective-permute-start.3
  35.7 0.6 collective-permute-done.2
  36.3 4.3 %collective-permute-done.3 = bf16[18,1,1024]{2,1,0:T(2,128)(2,1)S(1)} collective-permute-done((bf16[18,1,1024]{2,1,0:T(2,128)(2,1)S(1)}, bf16[18,1,1024]{2,1,0:T(2,128)(2,1)S(1)}, u32[]{:S(2)}, u32[]{:S(2)}) %collective-permute-start.3) | collective-permute-done | bytes 36896 | tf_op jit(solution)/shard_map/ppermute | solution.py:18
  40.6 1.6 maximum_maximum_fusion
  42.2 0.0 copy-start.6
  42.2 0.0 copy-start.2
  42.2 16.1 %fusion.35 = bf16[16,64,512]{2,1,0:T(8,128)(2,1)} fusion(bf16[16,64,1024]{2,1,0:T(8,128)(2,1)S(1)} %fusion.3, bf16[18,65,1024]{2,1,0:T(8,128)(2,1)S(1)} %get-tuple-element.6, bf16[1,64,1024]{2,1,0:T(8,128)(2,1)S(1)} %collective-permute-done.1, bf16[18,65,1024]{2,1,0:T(8,128)(2,1)S(1)} %get-tuple-element.5, ...), kind=kOutput, calls=%fused_computation.62 | convolution fusion | flops 1172832256 | bytes 17080320 | tf_op jit(solution)/shard_map/hwe,ec->hwc/dot_general | solution.py:110
  58.3 0.0 reduce-scatter.3.cloned.1.call-update
  58.3 0.0 all-gather.2.cloned.1.call-start
  58.4 0.1 dynamic_slice.7
  58.5 7.7 %reduce-scatter.3.cloned.1.call-done = bf16[16,64,256]{2,1,0:T(8,128)(2,1)} async-done(((bf16[16,64,512]{2,1,0:T(8,128)(2,1)}), bf16[16,64,256]{2,1,0:T(8,128)(2,1)}) %reduce-scatter.3.cloned.1.call-update) | async-done | bytes 524304 | tf_op jit(solution)/shard_map/reduce_scatter | solution.py:111
  66.2 1.2 add_convert_fusion.1
  67.4 19.6 %all_to_all.69 = bf16[8,2,16,4,256]{4,2,3,1,0:T(8,128)(2,1)S(1)} all-to-all(bf16[8,2,16,4,256]{4,2,3,1,0:T(8,128)(2,1)S(1)} %bitcast.80), channel_id=1, replica_groups=mesh['grp'=2,'gy'=4,'gx'=2,'ch'=2] {'gy'}, dimensions={0} | all-to-all | bytes 1048576 | tf_op jit(solution)/shard_map/all_to_all | solution.py:119
  87.1 0.3 copy.52
  87.4 10.0 %all_to_all.70 = bf16[2,8,16,4,256]{4,3,1,0,2:T(4,128)(2,1)S(1)} all-to-all(bf16[2,8,16,4,256]{4,3,1,0,2:T(4,128)(2,1)S(1)} %copy.52), channel_id=1, replica_groups=mesh['grp'=2,'gy'=4,'gx'=2,'ch'=2] {'gx'}, dimensions={2} | all-to-all | bytes 1048576 | tf_op jit(solution)/shard_map/all_to_all | solution.py:118
  97.4 0.3 copy.79
  97.7 0.1 copy.54
  97.8 0.9 copy.55
  98.7 0.0 all-gather.2.cloned.1.call-update
  98.7 0.2 reduce-scatter.5.cloned.1.call-start
  98.9 7.1 %all-gather.2.cloned.1.call-done = bf16[16,64,512]{2,1,0:T(8,128)(2,1)} async-done(((bf16[16,64,256]{2,1,0:T(8,128)(2,1)}), bf16[16,64,512]{2,1,0:T(8,128)(2,1)}) %all-gather.2.cloned.1.call-update) | async-done | bytes 1048592 | tf_op jit(solution)/shard_map/all_gather | solution.py:126
  106.0 1.4 convert_reduce_fusion
  107.5 1.7 fusion.26
  109.2 2.3 %fusion.34 = bf16[3,16,64,256]{3,2,0,1:T(8,128)(2,1)S(1)} fusion(bf16[16,64,512]{2,1,0:T(8,128)(2,1)} %all-gather.2.cloned.1.call-done, f32[512]{0:T(512)S(1)} %copy-done.10, f32[16,64]{1,0:T(8,128)S(1)} %add_rsqrt_fusion, f32[16,64]{1,0:T(8,128)S(1)} %broadcast_multiply_fusion, bf16[512,3,256]{2,0,1:T(8,128)(2,1)S(1)} %copy-done.8), kind=kOutput, calls=%fused_computation.61 | convolution fusion | flops 808714240 | bytes 3418112 | tf_op jit(solution)/shard_map/wtc,cke->kwte/dot_general | solution.py:73
  111.6 0.2 fusion.82
  111.7 1.3 copy.57
  113.1 0.5 copy.58
  113.6 1.3 copy.56
  114.9 4.9 %fusion.83 = (f32[16,8,64]{2,1,0:T(8,128)S(1)}, f32[16,8,64,64]{2,3,1,0:T(8,128)}) fusion(bf16[16,64,8,32]{1,3,2,0:T(8,128)(2,1)} %bitcast.91, bf16[16,64,8,32]{1,3,2,0:T(8,128)(2,1)S(1)} %bitcast.92), kind=kOutput, calls=%fused_computation.126 | convolution fusion | flops 35127360 | bytes 3178496 | tf_op jit(solution)/shard_map/sub | solution.py:84
  119.8 3.2 %fusion.33 = bf16[16,8,32,64]{3,2,1,0:T(8,128)(2,1)S(1)} fusion(bf16[16,64,8,32]{1,3,2,0:T(8,128)(2,1)} %bitcast.93, f32[16,8,64,64]{2,3,1,0:T(8,128)} %get-tuple-element.24, f32[16,8,64]{2,1,0:T(8,128)S(1)} %get-tuple-element.23), kind=kOutput, calls=%fused_computation.59 | convolution fusion | flops 34865152 | bytes 3178496 | tf_op jit(solution)/shard_map/whqk,wkhd->wqhd/dot_general | solution.py:85
  123.1 1.4 convolution_convert_fusion.1
  124.5 0.0 reduce-scatter.5.cloned.1.call-update
  124.5 9.8 %reduce-scatter.5.cloned.1.call-done = bf16[16,64,256]{2,1,0:T(8,128)(2,1)} async-done(((bf16[16,64,512]{2,1,0:T(8,128)(2,1)}), bf16[16,64,256]{2,1,0:T(8,128)(2,1)}) %reduce-scatter.5.cloned.1.call-update) | async-done | bytes 524304 | tf_op jit(solution)/shard_map/reduce_scatter | solution.py:131
  134.3 1.2 add_convert_fusion
  135.6 19.6 %all_to_all.71 = bf16[2,8,8,8,256]{4,3,2,0,1:T(8,128)(2,1)S(1)} all-to-all(bf16[2,8,8,8,256]{4,3,2,0,1:T(8,128)(2,1)S(1)} %bitcast.85), channel_id=1, replica_groups=mesh['grp'=2,'gy'=4,'gx'=2,'ch'=2] {'gy'}, dimensions={1} | all-to-all | bytes 1048576 | tf_op jit(solution)/shard_map/all_to_all | solution.py:137
  155.2 0.1 copy.64
  155.3 10.0 %all_to_all.72 = bf16[8,2,8,8,256]{4,2,1,0,3:T(8,128)(2,1)S(1)} all-to-all(bf16[8,2,8,8,256]{4,2,1,0,3:T(8,128)(2,1)S(1)} %copy.64), channel_id=1, replica_groups=mesh['grp'=2,'gy'=4,'gx'=2,'ch'=2] {'gx'}, dimensions={3} | all-to-all | bytes 1048576 | tf_op jit(solution)/shard_map/all_to_all | solution.py:136
  165.4 0.8 copy.67
  (27 shorter events, 0.3 us)
Async XLA Ops:
  6.5 1.2 copy-start
  6.5 29.1 %copy-start.4 = (bf16[3,3,1024]{2,1,0:T(4,128)(2,1)S(1)}, bf16[3,3,1024]{2,1,0:T(4,128)(2,1)}, u32[]{:S(2)}) copy-start(bf16[3,3,1024]{2,1,0:T(4,128)(2,1)} %param.14) | copy-start | bytes 55300
  6.5 59.6 %reduce-scatter.3.cloned.1.call-start = ((), (), s32[]{:S(2)}) async-start(), calls=%async_computation.6 | async-start | bytes 1572864 | tf_op jit(solution)/shard_map/reduce_scatter | solution.py:111
  18.9 7.7 %collective-permute-start = (bf16[1,64,1024]{2,1,0:T(8,128)(2,1)S(1)}, bf16[1,64,1024]{2,1,0:T(8,128)(2,1)S(1)}, u32[]{:S(2)}, u32[]{:S(2)}) collective-permute-start(bf16[1,64,1024]{2,1,0:T(8,128)(2,1)S(1)} %get-tuple-element.9), channel_id=1, source_target_pairs={{0,4},{4,8},{8,12},{1,5},{5,9},{9,13},{2,6},{6,10},{10,14},{3,7},{... | collective-permute-start | bytes 393224 | tf_op jit(solution)/shard_map/ppermute | solution.py:15
  23.8 6.9 %collective-permute-start.1 = (bf16[1,64,1024]{2,1,0:T(8,128)(2,1)S(1)}, bf16[1,64,1024]{2,1,0:T(8,128)(2,1)S(1)}, u32[]{:S(2)}, u32[]{:S(2)}) collective-permute-start(bf16[1,64,1024]{2,1,0:T(8,128)(2,1)S(1)} %get-tuple-element.10), channel_id=1, source_target_pairs={{4,0},{8,4},{12,8},{5,1},{9,5},{13,9},{6,2},{10,6},{14,10},{7,3},{... | collective-permute-start | bytes 393224 | tf_op jit(solution)/shard_map/ppermute | solution.py:18
  30.8 11.4 %copy-start.7 = (bf16[1024,512]{1,0:T(8,128)(2,1)S(1)}, bf16[1024,512]{1,0:T(8,128)(2,1)}, u32[]{:S(2)}) copy-start(bf16[1024,512]{1,0:T(8,128)(2,1)} %param.16) | copy-start | bytes 3145732
  30.8 11.4 %copy-start.9 = (f32[1024]{0:T(1024)S(1)}, f32[1024]{0:T(1024)}, u32[]{:S(2)}) copy-start(f32[1024]{0:T(1024)} %param.15) | copy-start | bytes 12292
  30.8 5.5 %collective-permute-start.2 = (bf16[18,1,1024]{2,1,0:T(2,128)(2,1)S(1)}, bf16[18,1,1024]{2,1,0:T(2,128)(2,1)S(1)}, u32[]{:S(2)}, u32[]{:S(2)}) collective-permute-start(bf16[18,1,1024]{2,1,0:T(2,128)(2,1)S(1)} %get-tuple-element.7), channel_id=1, source_target_pairs={{0,2},{1,3},{4,6},{5,7},{8,10},{9,11},{12,14},{13,15},{16,18},{17,... | collective-permute-start | bytes 110600 | tf_op jit(solution)/shard_map/ppermute | solution.py:15
  34.4 6.2 %collective-permute-start.3 = (bf16[18,1,1024]{2,1,0:T(2,128)(2,1)S(1)}, bf16[18,1,1024]{2,1,0:T(2,128)(2,1)S(1)}, u32[]{:S(2)}, u32[]{:S(2)}) collective-permute-start(bf16[18,1,1024]{2,1,0:T(2,128)(2,1)S(1)} %get-tuple-element.8), channel_id=1, source_target_pairs={{2,0},{3,1},{6,4},{7,5},{10,8},{11,9},{14,12},{15,13},{18,16},{19,... | collective-permute-start | bytes 110600 | tf_op jit(solution)/shard_map/ppermute | solution.py:18
  42.2 16.2 %copy-start.6 = (f32[512]{0:T(512)S(1)}, f32[512]{0:T(512)}, u32[]{:S(2)}) copy-start(f32[512]{0:T(512)} %param.17) | copy-start | bytes 6148
  42.2 24.0 %copy-start.2 = (bf16[16,64,512]{2,1,0:T(8,128)(2,1)S(1)}, bf16[16,64,512]{2,1,0:T(8,128)(2,1)}, u32[]{:S(2)}) copy-start(bf16[16,64,512]{2,1,0:T(8,128)(2,1)} %param.11) | copy-start | bytes 3145732
  58.3 47.7 %all-gather.2.cloned.1.call-start = ((), (), s32[]{:S(2)}) async-start(), calls=%async_computation.7 | async-start | bytes 1572864 | tf_op jit(solution)/shard_map/all_gather | solution.py:126
  87.1 22.1 %copy-start.8 = (bf16[512,3,256]{2,0,1:T(8,128)(2,1)S(1)}, bf16[512,3,256]{2,0,1:T(8,128)(2,1)}, u32[]{:S(2)}) copy-start(bf16[512,3,256]{2,0,1:T(8,128)(2,1)} %param.19) | copy-start | bytes 2359300
  87.1 22.1 %copy-start.10 = (f32[512]{0:T(512)S(1)}, f32[512]{0:T(512)}, u32[]{:S(2)}) copy-start(f32[512]{0:T(512)} %param.18) | copy-start | bytes 6148
  98.7 35.6 %reduce-scatter.5.cloned.1.call-start = ((), (), s32[]{:S(2)}) async-start(), calls=%async_computation.8 | async-start | bytes 1572864 | tf_op jit(solution)/shard_map/reduce_scatter | solution.py:131
  119.8 3.3 %copy-start.3 = (bf16[256,512]{1,0:T(8,128)(2,1)S(1)}, bf16[256,512]{1,0:T(8,128)(2,1)}, u32[]{:S(2)}) copy-start(bf16[256,512]{1,0:T(8,128)(2,1)} %param.20) | copy-start | bytes 786436
  119.8 14.5 %copy-start.1 = (bf16[1,2,1,8,8,8,256]{6,5,4,3,1,2,0:T(8,128)(2,1)S(1)}, bf16[1,2,1,8,8,8,256]{6,5,4,3,1,2,0:T(8,128)(2,1)}, u32[]{:S(2)}) copy-start(bf16[1,2,1,8,8,8,256]{6,5,4,3,1,2,0:T(8,128)(2,1)} %copy.55) | copy-start | bytes 1572868
  119.8 14.5 %copy-start.5 = (f32[256]{0:T(256)S(1)}, f32[256]{0:T(256)}, u32[]{:S(2)}) copy-start(f32[256]{0:T(256)} %param.21) | copy-start | bytes 3076
Sparse Core Ops, SparseCore 0:
  58.5 7.6 reduce-scatter.2
  98.8 7.1 all-gather.1
  124.7 9.5 reduce-scatter.4
where the time goes:
time: 173 us
  blocking collectives  59.2 us (34%)
  matrix products  39 us (23%)
  waiting for transfers between devices  35.1 us (20%)
  between operations  13.4 us (8%)
  starting transfers between devices  11.4 us (7%)
  local copies, waits for them, and re-layouts  7.33 us (4%)
  other arithmetic  7.27 us (4%)
    all_to_all x1, blocking collectives, per_device(): lax.all_to_all(arranged, 'gy', split_axis=0, concat_axis=1, tiled=True)  19.6 us
    all_to_all x1, blocking collectives, per_device(): lax.all_to_all(leaving, 'gy', split_axis=1, concat_axis=0, tiled=True)  19.6 us
    dot_general x1, matrix products, per_device(): jnp.einsum('hwe,ec->hwc', depth, w_project, preferred_element_type=jnp.fl...  16.1 us
    dot_general x1, matrix products, expand_cells(): jnp.einsum('hwc,ce->hwe', source, w_expand, preferred_element_type=jnp.fl...  11.1 us
    all_to_all x1, blocking collectives, per_device(): lax.all_to_all(lax.all_to_all(leaving, 'gy', split_axis=1, concat_axis=0,...  10 us
    all_to_all x1, blocking collectives, per_device(): lax.all_to_all(lax.all_to_all(arranged, 'gy', split_axis=0, concat_axis=1...  10 us
    reduce_scatter x1, waiting for transfers between devices, per_device(): lax.psum_scatter(attention_terms.astype(jnp.bfloat16), 'ch', scatter_dime...  9.76 us
    ppermute x2, starting transfers between devices, extended(): lax.ppermute(lax.slice_in_dim(block, block.shape[dim] - width, None, axis...  8.51 us
  transfers between devices with their start and end apart: 7, of which 7 were waited for; matrix products, arithmetic and copies ran while one was open for 0% of the time, Pallas kernels for 0%

commit v1 on v0

v1 whole, which is shorter than its diff:
```python
import functools

import jax
import jax.numpy as jnp
import numpy as np
from jax import lax
from jax.experimental import pallas as pl
from jax.experimental.pallas import tpu as pltpu
from jax.sharding import PartitionSpec as P

HEAD_DIM = 32
GRID = 8
MESH = pl.DeviceIdType.MESH
F32 = jnp.float32
BF16 = jnp.bfloat16


def gelu(v):
    return v * (0.5 * (1.0 + lax.erf(v * np.float32(np.sqrt(0.5)))))


def dot(a, b):
    return jnp.dot(a, b, preferred_element_type=F32)


class Plan:
    def __init__(self, mesh_shape, tile_h, tile_w):
        self.n_rows, self.n_cols = mesh_shape["gy"], mesh_shape["gx"]
        self.tile_h, self.tile_w = tile_h, tile_w
        stride_h = tile_h * self.n_rows // GRID
        stride_w = tile_w * self.n_cols // GRID
        self.depth_h, self.depth_w = min(tile_h, stride_h), min(tile_w, stride_w)
        self.steps_h, self.steps_w = stride_h // self.depth_h, stride_w // self.depth_w
        self.n_i, self.n_j = tile_h // self.depth_h, tile_w // self.depth_w
        self.ph, self.pw = GRID // self.n_i, GRID // self.n_j
        self.own_h, self.own_w = self.depth_h // self.ph, self.depth_w // self.pw
        assert self.own_h == 2
        self.n_t = self.n_i * self.n_j
        self.sources = self.ph * self.pw
        self.piece = self.own_w * self.n_t
        self.slab = self.n_i * tile_w
        groups = self.own_w
        while groups > 1 and (self.piece // groups) % 16:
            groups //= 2
        self.groups = groups
        self.span = self.piece // groups

    def permutation(self):
        out = np.zeros((self.slab, self.slab), np.float32)
        for q in range(self.pw):
            for b in range(self.own_w):
                for i in range(self.n_i):
                    for j in range(self.n_j):
                        row = (q * self.own_w + b) * self.n_t + i * self.n_j + j
                        out[row, i * self.tile_w + j * self.depth_w + q * self.own_w + b] = 1
        return out

    def score_bias(self):
        rows = np.arange(self.sources * self.span)
        window = (rows % self.span) // self.n_t
        return np.where(window[:, None] == window[None, :], 0.0, -1e30).astype(np.float32)


def kernel(
    plan, cells, w_exp, b_exp, w_dep, b_dep, w_proj, b_proj, gain, w_qkv, w_out, b_out,
    perm, perm_t, bias_s, edge_own, out,
    exp, halo, edge, colin, colexp, dbuf, psend, precv, acc, fsend, frecv,
    wq_other, wo_other, bo_full, osend, oin,
    halo_s, halo_r, col_s, col_r, w_s, w_r, p_s, p_r, f_s, f_r, o_s, o_r,
):
    tile_h, tile_w = plan.tile_h, plan.tile_w
    width = cells.shape[2]
    inner = w_exp.shape[1]
    half = width // 2
    z, x, c = lax.axis_index("gy"), lax.axis_index("gx"), lax.axis_index("ch")
    zs, xs = lax.rem(z, plan.steps_h), lax.rem(x, plan.steps_w)
    mp, mq = lax.div(z, plan.steps_h), lax.div(x, plan.steps_w)
    my_s = mp * plan.pw + mq
    last_z, last_x = plan.n_rows - 1, plan.n_cols - 1
    partner = {"ch": 1 - c}
    has_top, has_bot = z > 0, z < last_z
    has_left, has_right = x > 0, x < last_x

    def peer(s, core):
        p, q = lax.div(s, plan.pw), lax.rem(s, plan.pw)
        return {"gy": p * plan.steps_h + zs, "gx": q * plan.steps_w + xs, "ch": core}

    def remote(src, dst, send, recv, device):
        return pltpu.make_async_remote_copy(
            src_ref=src, dst_ref=dst, send_sem=send, recv_sem=recv,
            device_id=device, device_id_type=MESH,
        )

    barrier = pltpu.get_barrier_semaphore()
    around = (
        (has_top, {"gy": jnp.maximum(z - 1, 0)}),
        (has_bot, {"gy": jnp.minimum(z + 1, last_z)}),
        (has_left, {"gx": jnp.maximum(x - 1, 0)}),
        (has_right, {"gx": jnp.minimum(x + 1, last_x)}),
    )
    count = jnp.int32(2 * plan.sources - 1)
    for there, device in around:
        @pl.when(there)
        def _():
            pl.semaphore_signal(barrier, inc=1, device_id=device, device_id_type=MESH)
        count = count + there.astype(jnp.int32)

    @pl.loop(0, 2 * plan.sources)
    def _(t):
        s, core = lax.div(t, 2), lax.rem(t, 2)

        @pl.when(jnp.logical_not((s == my_s) & (core == c)))
        def _():
            pl.semaphore_signal(barrier, inc=1, device_id=peer(s, core), device_id_type=MESH)

    pl.semaphore_wait(barrier, count)

    down = remote(cells.at[tile_h - 1], halo.at[0], halo_s.at[0], halo_r.at[0], around[1][1])
    up = remote(cells.at[0], halo.at[1], halo_s.at[1], halo_r.at[1], around[0][1])
    rightward = remote(edge.at[1], colin.at[0], col_s.at[0], col_r.at[0], around[3][1])
    leftward = remote(edge.at[0], colin.at[1], col_s.at[1], col_r.at[1], around[2][1])
    weights = (
        remote(w_qkv, wq_other, w_s.at[0], w_r.at[0], partner),
        remote(w_out, wo_other, w_s.at[1], w_r.at[1], partner),
        remote(b_out, bo_full.at[c], w_s.at[2], w_r.at[2], partner),
    )

    @pl.when(has_bot)
    def _():
        down.start()

    @pl.when(has_top)
    def _():
        up.start()

    for copy in weights:
        copy.start()
    bo_full[c] = b_out[...]

    lanes_e = 256
    rows_e = 4

    def expand(source, lanes):
        return gelu(dot(source, w_exp[:, lanes]) + b_exp[:, lanes])

    def expand_rows(first):
        source = cells[pl.ds(first, rows_e)].reshape(rows_e * tile_w, width)

        @pl.loop(0, inner // lanes_e)
        def _(t):
            lanes = pl.ds(pl.multiple_of(t * lanes_e, lanes_e), lanes_e)
            value = expand(source, lanes)
            for r in range(rows_e):
                exp[first + 1 + r, 0:tile_w, lanes] = value[r * tile_w : (r + 1) * tile_w]

    @pl.loop(0, tile_h // rows_e // 2)
    def _(t):
        expand_rows(t * rows_e)

    for index, there, copy in ((0, has_top, down), (1, has_bot, up)):
        @pl.when(there)
        def _():
            copy.wait_recv()

        @pl.when(jnp.logical_not(there))
        def _():
            halo[index] = jnp.zeros(halo.shape[1:], BF16)

    flat = cells[...].reshape(tile_h * tile_w, width)
    span_rows = edge.shape[1]
    picked = dot(edge_own[...], flat)
    at_row = lax.broadcasted_iota(jnp.int32, (span_rows, width), 0)
    for side, col in ((0, 0), (1, tile_w - 1)):
        top = halo[0].astype(F32)[col : col + 1]
        bottom = halo[1].astype(F32)[col : col + 1]
        value = picked[side * span_rows : (side + 1) * span_rows]
        value = jnp.where(at_row == 0, top, jnp.where(at_row == tile_h + 1, bottom, value))
        edge[side] = value.astype(BF16)

    @pl.when(has_right)
    def _():
        rightward.start()

    @pl.when(has_left)
    def _():
        leftward.start()

    @pl.loop(tile_h // rows_e // 2, tile_h // rows_e)
    def _(t):
        expand_rows(t * rows_e)

    ok_top, ok_bot = has_top.astype(F32), has_bot.astype(F32)
    ok_left, ok_right = has_left.astype(F32), has_right.astype(F32)
    halo_flat = halo[...].reshape(2 * tile_w, width)

    @pl.loop(0, inner // lanes_e)
    def _(t):
        lanes = pl.ds(pl.multiple_of(t * lanes_e, lanes_e), lanes_e)
        value = expand(halo_flat, lanes)
        exp[0, 0:tile_w, lanes] = value[:tile_w] * ok_top
        exp[tile_h + 1, 0:tile_w, lanes] = value[tile_w:] * ok_bot

    for index, there, copy in ((0, has_left, rightward), (1, has_right, leftward)):
        @pl.when(there)
        def _():
            copy.wait_recv()

        @pl.when(jnp.logical_not(there))
        def _():
            colin[index] = jnp.zeros(colin.shape[1:], BF16)

    col_flat = colin[...].reshape(2 * span_rows, width)

    @pl.loop(0, inner // lanes_e)
    def _(t):
        lanes = pl.ds(pl.multiple_of(t * lanes_e, lanes_e), lanes_e)
        colexp[:, lanes] = expand(col_flat, lanes)

    @pl.loop(0, tile_h + 2)
    def _(r):
        row_ok = jnp.where(r == 0, ok_top, jnp.where(r == tile_h + 1, ok_bot, jnp.float32(1)))
        left = colexp[pl.ds(r, 1), :] * (row_ok * ok_left)
        right = colexp[pl.ds(span_rows + r, 1), :] * (row_ok * ok_right)
        at = lax.broadcasted_iota(jnp.int32, (8, inner), 0)
        exp[r, tile_w : tile_w + 8, :] = jnp.where(at == 0, right, left)

    lanes_d = 128
    wide = tile_w + 8

    def partial_copy(p):
        return remote(psend.at[p], precv.at[p], p_s.at[p], p_r.at[p], partner)

    def depth_rows(p):
        @pl.loop(0, 2 * plan.n_i * (inner // lanes_d))
        def _(t):
            chunk = lax.rem(t, inner // lanes_d)
            which = lax.div(t, inner // lanes_d)
            i, kk = lax.rem(which, plan.n_i), lax.div(which, plan.n_i)
            k = jnp.where(kk == 0, 1 - c, c)
            row = i * plan.depth_h + 2 * p + k
            lanes = pl.ds(pl.multiple_of(chunk * lanes_d, lanes_d), lanes_d)
            e = [exp[row + di, :, lanes] for di in range(3)]
            sums = []
            for dj in range(3):
                total = e[0] * w_dep[dj : dj + 1, lanes]
                for di in (1, 2):
                    total = total + e[di] * w_dep[3 * di + dj : 3 * di + dj + 1, lanes]
                sums.append(total)
            summed = (
                pltpu.roll(sums[0], 1, 0)[:tile_w]
                + sums[1][:tile_w]
                + pltpu.roll(sums[2], wide - 1, 0)[:tile_w]
            )
            value = gelu(summed + b_dep[:, lanes]).astype(BF16)
            dbuf[kk, pl.ds(pl.multiple_of(i * tile_w, tile_w), tile_w), lanes] = value

        psend[p] = dot(dbuf[0], w_proj[...]).astype(BF16)
        partial_copy(p).start()
        acc[p] = dot(dbuf[1], w_proj[...])

    def forward_copy(p, q):
        s = p * plan.pw + q
        return remote(fsend.at[p, q], frecv.at[my_s], f_s.at[s], f_r.at[my_s], peer(s, c))

    def finish(p):
        partial_copy(p).wait_recv()
        own = jnp.concatenate(
            [cells[i * plan.depth_h + 2 * p + c] for i in range(plan.n_i)], axis=0
        )
        mixed = own.astype(F32) + acc[p] + precv[p].astype(F32) + b_proj[...]
        moved = dot(perm[...], mixed.astype(BF16)).astype(BF16)
        for q in range(plan.pw):
            s = p * plan.pw + q
            value = moved[q * plan.piece : (q + 1) * plan.piece]
            fsend[p, q] = value

            @pl.when(s == my_s)
            def _():
                frecv[my_s] = value

            @pl.when(s != my_s)
            def _():
                forward_copy(p, q).start()

    def step_peer(t):
        return lax.rem(mp + 1 + t, plan.ph)

    depth_rows(step_peer(0))

    @pl.loop(1, plan.ph)
    def _(t):
        depth_rows(step_peer(t))
        finish(step_peer(t - 1))

    finish(step_peer(plan.ph - 1))

    for copy in weights:
        copy.wait_recv()

    @pl.loop(0, plan.sources)
    def _(s):
        @pl.when(s != my_s)
        def _():
            remote(fsend.at[0, 0], frecv.at[s], f_s.at[s], f_r.at[s], partner).wait_recv()

    tokens = plan.sources * plan.span
    heads = half // HEAD_DIM
    lane = lax.broadcasted_iota(jnp.int32, (1, half), 1)
    head_masks = [
        ((lane >= h * HEAD_DIM) & (lane < (h + 1) * HEAD_DIM)).astype(F32) for h in range(heads)
    ]

    def return_copy(g, s, side):
        rows = pl.ds(g * plan.span, plan.span)
        return remote(
            osend.at[side, s, rows], oin.at[c, my_s, rows],
            o_s.at[side, s, g], o_r.at[c, my_s, g], peer(s, side),
        )

    for g in range(plan.groups):
        rows = slice(g * plan.span, (g + 1) * plan.span)
        mixed = frecv[:, rows, :].astype(F32).reshape(tokens, width)
        centered = mixed - jnp.mean(mixed, axis=-1, keepdims=True)
        spread = jnp.mean(centered * centered, axis=-1, keepdims=True)
        normed = (centered * lax.rsqrt(spread + 1e-05) * gain[...]).astype(BF16)
        total = mixed
        for wq, wo in ((w_qkv, w_out), (wq_other, wo_other)):
            query = dot(normed, wq[0]).astype(BF16)
            keyset = dot(normed, wq[1]).astype(BF16)
            valueset = dot(normed, wq[2]).astype(BF16)
            stacked = jnp.concatenate([query * m.astype(BF16) for m in head_masks], axis=0)
            scores = lax.dot_general(
                stacked, keyset, (((1,), (1,)), ((), ())), preferred_element_type=F32
            )
            scores = scores.reshape(heads, tokens, tokens) * HEAD_DIM ** (-0.5) + bias_s[...]
            top = jnp.max(scores, axis=-1, keepdims=True)
            weights_e = jnp.exp(scores - top)
            weights_e = weights_e / jnp.sum(weights_e, axis=-1, keepdims=True)
            mixed_v = dot(weights_e.astype(BF16).reshape(heads * tokens, tokens), valueset)
            attended = mixed_v[:tokens] * head_masks[0]
            for h in range(1, heads):
                attended = attended + mixed_v[h * tokens : (h + 1) * tokens] * head_masks[h]
            total = total + dot(attended.astype(BF16), wo[...])
        for side in range(2):
            lanes = slice(side * half, (side + 1) * half)
            value = (total[:, lanes] + bo_full[side]).astype(BF16)
            value = value.reshape(plan.sources, plan.span, half)
            osend[side, :, rows, :] = value

            @pl.when(side == c)
            def _():
                oin[c, my_s, rows] = osend[side, my_s, rows]

        @pl.loop(0, 2 * plan.sources)
        def _(t):
            s, side = lax.div(t, 2), lax.rem(t, 2)

            @pl.when(jnp.logical_not((s == my_s) & (side == c)))
            def _():
                return_copy(g, s, side).start()

    @pl.loop(0, 2 * plan.ph)
    def _(t):
        p, core = lax.div(t, 2), lax.rem(t, 2)
        for q in range(plan.pw):
            s = p * plan.pw + q

            @pl.when(jnp.logical_not((s == my_s) & (core == c)))
            def _():
                for g in range(plan.groups):
                    rows = pl.ds(g * plan.span, plan.span)
                    remote(
                        osend.at[0, 0, rows], oin.at[core, s, rows],
                        o_s.at[0, 0, g], o_r.at[core, s, g], partner,
                    ).wait_recv()
        arrived = oin[core, pl.ds(p * plan.pw, plan.pw)]
        arrived = arrived.astype(F32).reshape(plan.slab, half).astype(BF16)
        placed = dot(perm_t[...], arrived).astype(BF16)
        for i in range(plan.n_i):
            out[i * plan.depth_h + 2 * p + core] = placed[i * tile_w : (i + 1) * tile_w]

    @pl.when(has_bot)
    def _():
        down.wait_send()

    @pl.when(has_top)
    def _():
        up.wait_send()

    @pl.when(has_right)
    def _():
        rightward.wait_send()

    @pl.when(has_left)
    def _():
        leftward.wait_send()

    for copy in weights:
        copy.wait_send()

    @pl.loop(0, plan.ph)
    def _(p):
        partial_copy(p).wait_send()
        for q in range(plan.pw):
            @pl.when(p * plan.pw + q != my_s)
            def _():
                forward_copy(p, q).wait_send()

    @pl.loop(0, 2 * plan.sources)
    def _(t):
        s, side = lax.div(t, 2), lax.rem(t, 2)

        @pl.when(jnp.logical_not((s == my_s) & (side == c)))
        def _():
            for g in range(plan.groups):
                return_copy(g, s, side).wait_send()


def per_device(
    mesh_shape, cells, w_expand, b_expand, w_depth, b_depth, w_project, b_project, ln_gain,
    w_qkv, w_out, b_out,
):
    tile_h, tile_w, width = cells.shape
    plan = Plan(mesh_shape, tile_h, tile_w)
    inner = w_expand.shape[1]
    half = width // 2
    span_rows = -(-(tile_h + 2) // 16) * 16
    edge_own = np.zeros((2 * span_rows, tile_h * tile_w), np.float32)
    for r in range(tile_h):
        edge_own[1 + r, r * tile_w] = 1
        edge_own[span_rows + 1 + r, r * tile_w + tile_w - 1] = 1
    perm = plan.permutation()
    args = (
        cells, w_expand, b_expand[None], w_depth.reshape(9, inner).astype(F32), b_depth[None],
        w_project, b_project[None], ln_gain[None], w_qkv.transpose(1, 0, 2), w_out, b_out[None],
        jnp.asarray(perm, BF16), jnp.asarray(perm.T, BF16),
        jnp.asarray(plan.score_bias()), jnp.asarray(edge_own, BF16),
    )
    dma = pltpu.SemaphoreType.DMA
    vmem = pltpu.VMEM
    n = plan
    return pl.pallas_call(
        functools.partial(kernel, plan),
        out_shape=jax.ShapeDtypeStruct((tile_h, tile_w, half), BF16),
        in_specs=[pl.BlockSpec(memory_space=pltpu.VMEM)] * len(args),
        out_specs=pl.BlockSpec(memory_space=pltpu.VMEM),
        scratch_shapes=[
            vmem((tile_h + 2, tile_w + 8, inner), F32),
            vmem((2, tile_w, width), BF16),
            vmem((2, span_rows, width), BF16),
            vmem((2, span_rows, width), BF16),
            vmem((2 * span_rows, inner), F32),
            vmem((2, n.slab, inner), BF16),
            vmem((n.ph, n.slab, width), BF16),
            vmem((n.ph, n.slab, width), BF16),
            vmem((n.ph, n.slab, width), F32),
            vmem((n.ph, n.pw, n.piece, width), BF16),
            vmem((n.sources, n.piece, width), BF16),
            vmem((3, width, half), BF16),
            vmem((half, width), BF16),
            vmem((2, 1, half), F32),
            vmem((2, n.sources, n.piece, half), BF16),
            vmem((2, n.sources, n.piece, half), BF16),
            dma((2,)), dma((2,)), dma((2,)), dma((2,)), dma((3,)), dma((3,)),
            dma((n.ph,)), dma((n.ph,)), dma((n.sources,)), dma((n.sources,)),
            dma((2, n.sources, n.groups)), dma((2, n.sources, n.groups)),
        ],
        compiler_params=pltpu.CompilerParams(
            collective_id=0, has_side_effects=True, vmem_limit_bytes=60 << 20
        ),
    )(*args)


def solution(mesh):
    placed = (
        P(("grp", "gy"), "gx", None),
        P(None, "ch"),
        P("ch"),
        P(None, None, "ch"),
        P("ch"),
        P("ch", None),
        P(),
        P(),
        P(None, None, "ch"),
        P("ch", None),
        P("ch"),
    )
    return jax.shard_map(
        functools.partial(per_device, dict(mesh.shape)),
        mesh=mesh,
        in_specs=placed,
        out_specs=P(("grp", "gy"), "gx", "ch"),
        check_vma=False,
    )
```

time: 173 us -> 55.9 us (0.32)
  blocking collectives: 59.2 us -> 0 us
  Pallas kernels: 0 us -> 52.4 us
  matrix products: 39 us -> 0 us
  waiting for transfers between devices: 35.1 us -> 0 us
  between operations: 13.4 us -> 0.01 us
  starting transfers between devices: 11.4 us -> 0 us
  other arithmetic: 7.27 us -> 0 us
  local copies, waits for them, and re-layouts: 7.33 us -> 3.26 us
    all_to_all x4 -> x0, blocking collectives: 59.2 us -> none  [the longest x1 19.6 us: per_device(): lax.all_to_all(arranged, 'gy', split_axis=0, concat_axis=1, tiled=True)]
    pallas_call x0 -> x1, Pallas kernels: none -> 52.4 us  [per_device(): pl.pallas_call(functools.partial(kernel, plan), out_shape=jax.ShapeDtypeS...]
    dot_general x5 -> x0, matrix products: 34.1 us -> none  [the longest x1 16.1 us: per_device(): jnp.einsum('hwe,ec->hwc', depth, w_project, preferred_element_type=jnp.fl...]
    reduce_scatter x2 -> x0, waiting for transfers between devices: 17.5 us -> none  [the longest x1 9.76 us: per_device(): lax.psum_scatter(attention_terms.astype(jnp.bfloat16), 'ch', scatter_dime...]
    ppermute x4 -> x0, starting transfers between devices: 11.1 us -> none  [the longest x2 8.51 us: extended(): lax.ppermute(lax.slice_in_dim(block, block.shape[dim] - width, None, axis...]
    ppermute x4 -> x0, waiting for transfers between devices: 10.5 us -> none  [the longest x2 8.42 us: extended(): lax.ppermute(lax.slice_in_dim(block, 0, width, axis=dim), axis, backward)]
    all_gather x1 -> x0, waiting for transfers between devices: 7.12 us -> none  [per_device(): window_full = lax.all_gather(window_own, 'ch', axis=2, tiled=True)]
    sub x1 -> x0, matrix products: 4.92 us -> none  [attend(): weights = jax.nn.softmax(scores, axis=-1).astype(jnp.bfloat16)]
  transfers between devices with their start and end apart: 7 -> 0, of which waited for: 7 -> 0; matrix products, arithmetic and copies ran while one was open for 0% -> 0% of each run, Pallas kernels for 0% -> 0%
where the time goes in v1:
time: 55.9 us; the launch traced here: 55.7 us
  Pallas kernels  52.4 us (94%)
  local copies, waits for them, and re-layouts  3.26 us (6%)
    pallas_call x1, Pallas kernels, per_device(): pl.pallas_call(functools.partial(kernel, plan), out_shape=jax.ShapeDtypeS...  52.4 us
    unnamed x1, local copies, waits for them, and re-layouts  1.88 us
    convert_element_type x1, local copies, waits for them, and re-layouts, per_device(): w_depth.reshape(9, inner).astype(F32)  1.38 us

profile of v1, /device:TPU:0, one launch (start us, length us, event | category | flops | bytes accessed | tf_op | source)
XLA Modules:
  0.0 55.7 jit_solution(10762810913780088974)
XLA Ops:
  0.0 1.4 %reshape.3.w_dep = f32[9,1024]{1,0:T(8,128)} reshape(bf16[3,3,1024]{2,1,0:T(4,128)(2,1)} %param.18) | data formatting | bytes 55296 | tf_op jit(solution)/shard_map/convert_element_type | solution.py:434
  1.4 52.4 %shard_map.145 = bf16[16,64,256]{2,1,0:T(8,128)(2,1)} custom-call(bf16[16,64,512]{2,1,0:T(8,128)(2,1)} %cells.1, bf16[512,1024]{1,0:T(8,128)(2,1)} %w_exp.1, f32[1,1024]{1,0:T(1,128)} %bitcast.7, f32[9,1024]{1,0:T(8,128)} %reshape.3.w_dep, f32[1,1024]{1,0:T(1,128)} %bitcast.8, bf16[1024,512]{1,0:T(8,128)(2,1)} %w_proj.1, f32[1,512]{1,0:T(1,128)} %bitcast.9, ...), custom_call_target="tpu_custom_call" | custom-call | tf_op jit(solution)/shard_map/pallas_call | solution.py:442
  53.8 1.9 %copy.17 = bf16[16,64,256]{2,1,0:T(8,128)(2,1)} copy(bf16[16,64,256]{2,1,0:T(8,128)(2,1)} %shard_map.145) | data formatting | bytes 1048576

commit v2 on v1

--- a/solution.py
+++ b/solution.py
@@ -37,9 +37,10 @@
         assert self.own_h == 2
         self.n_t = self.n_i * self.n_j
         self.sources = self.ph * self.pw
-        self.piece = self.own_w * self.n_t
+        self.part_w = self.own_w // 2
+        self.piece = self.part_w * self.n_t
         self.slab = self.n_i * tile_w
-        groups = self.own_w
+        groups = self.part_w
         while groups > 1 and (self.piece // groups) % 16:
             groups //= 2
         self.groups = groups
@@ -47,12 +48,15 @@
 
     def permutation(self):
         out = np.zeros((self.slab, self.slab), np.float32)
+        half = self.slab // 2
         for q in range(self.pw):
             for b in range(self.own_w):
+                core, b_in = b // self.part_w, b % self.part_w
                 for i in range(self.n_i):
                     for j in range(self.n_j):
-                        row = (q * self.own_w + b) * self.n_t + i * self.n_j + j
-                        out[row, i * self.tile_w + j * self.depth_w + q * self.own_w + b] = 1
+                        row = (q * self.part_w + b_in) * self.n_t + i * self.n_j + j
+                        column = j * self.depth_w + q * self.own_w + b
+                        out[core * half + row, i * self.tile_w + column] = 1
         return out
 
     def score_bias(self):
@@ -62,15 +66,17 @@
 
 
 def kernel(
-    plan, cells, w_exp, b_exp, w_dep, b_dep, w_proj, b_proj, gain, w_qkv, w_out, b_out,
-    perm, perm_t, bias_s, edge_own, out,
-    exp, halo, edge, colin, colexp, dbuf, psend, precv, acc, fsend, frecv,
+    plan, cells_h, w_exp_h, b_exp, w_dep_in, b_dep, w_proj_h, b_proj, gain, w_qkv_h, w_out_h,
+    b_out, perm, perm_t, bias_s, edge_own, out,
+    cells, w_exp, w_proj, w_qkv, w_out, w_dep,
+    exp, halo, edge, colin, colexp, dbuf, dperm, psend, precv, acc, fsend, frecv,
     wq_other, wo_other, bo_full, osend, oin,
-    halo_s, halo_r, col_s, col_r, w_s, w_r, p_s, p_r, f_s, f_r, o_s, o_r,
+    in_s, halo_s, halo_r, col_s, col_r, w_s, w_r, p_s, p_r, f_s, f_r, o_s, o_r,
 ):
     tile_h, tile_w = plan.tile_h, plan.tile_w
     width = cells.shape[2]
     inner = w_exp.shape[1]
+    part = plan.slab // 2
     half = width // 2
     z, x, c = lax.axis_index("gy"), lax.axis_index("gx"), lax.axis_index("ch")
     zs, xs = lax.rem(z, plan.steps_h), lax.rem(x, plan.steps_w)
@@ -90,6 +96,16 @@
             src_ref=src, dst_ref=dst, send_sem=send, recv_sem=recv,
             device_id=device, device_id_type=MESH,
         )
+
+    loads = [
+        pltpu.make_async_copy(src, dst, in_s.at[n])
+        for n, (src, dst) in enumerate((
+            (cells_h, cells), (w_exp_h, w_exp), (w_proj_h, w_proj), (w_qkv_h, w_qkv),
+            (w_out_h, w_out),
+        ))
+    ]
+    for load in loads:
+        load.start()
 
     barrier = pltpu.get_barrier_semaphore()
     around = (
@@ -113,29 +129,21 @@
         def _():
             pl.semaphore_signal(barrier, inc=1, device_id=peer(s, core), device_id_type=MESH)
 
-    pl.semaphore_wait(barrier, count)
-
-    down = remote(cells.at[tile_h - 1], halo.at[0], halo_s.at[0], halo_r.at[0], around[1][1])
-    up = remote(cells.at[0], halo.at[1], halo_s.at[1], halo_r.at[1], around[0][1])
+    down = remote(cells_h.at[tile_h - 1], halo.at[0], halo_s.at[0], halo_r.at[0], around[1][1])
+    up = remote(cells_h.at[0], halo.at[1], halo_s.at[1], halo_r.at[1], around[0][1])
     rightward = remote(edge.at[1], colin.at[0], col_s.at[0], col_r.at[0], around[3][1])
     leftward = remote(edge.at[0], colin.at[1], col_s.at[1], col_r.at[1], around[2][1])
     weights = (
-        remote(w_qkv, wq_other, w_s.at[0], w_r.at[0], partner),
-        remote(w_out, wo_other, w_s.at[1], w_r.at[1], partner),
+        remote(w_qkv_h, wq_other, w_s.at[0], w_r.at[0], partner),
+        remote(w_out_h, wo_other, w_s.at[1], w_r.at[1], partner),
         remote(b_out, bo_full.at[c], w_s.at[2], w_r.at[2], partner),
     )
 
-    @pl.when(has_bot)
-    def _():
-        down.start()
-
-    @pl.when(has_top)
-    def _():
-        up.start()
-
-    for copy in weights:
-        copy.start()
+    for di in range(3):
+        w_dep[3 * di : 3 * di + 3] = w_dep_in[di].astype(F32)
     bo_full[c] = b_out[...]
+    loads[0].wait()
+    loads[1].wait()
 
     lanes_e = 256
     rows_e = 4
@@ -153,7 +161,21 @@
             for r in range(rows_e):
                 exp[first + 1 + r, 0:tile_w, lanes] = value[r * tile_w : (r + 1) * tile_w]
 
-    @pl.loop(0, tile_h // rows_e // 2)
+    expand_rows(0)
+    pl.semaphore_wait(barrier, count)
+
+    @pl.when(has_bot)
+    def _():
+        down.start()
+
+    @pl.when(has_top)
+    def _():
+        up.start()
+
+    for copy in weights:
+        copy.start()
+
+    @pl.loop(1, tile_h // rows_e)
     def _(t):
         expand_rows(t * rows_e)
 
@@ -185,10 +207,6 @@
     def _():
         leftward.start()
 
-    @pl.loop(tile_h // rows_e // 2, tile_h // rows_e)
-    def _(t):
-        expand_rows(t * rows_e)
-
     ok_top, ok_bot = has_top.astype(F32), has_bot.astype(F32)
     ok_left, ok_right = has_left.astype(F32), has_right.astype(F32)
     halo_flat = halo[...].reshape(2 * tile_w, width)
@@ -227,16 +245,18 @@
     lanes_d = 128
     wide = tile_w + 8
 
-    def partial_copy(p):
-        return remote(psend.at[p], precv.at[p], p_s.at[p], p_r.at[p], partner)
-
-    def depth_rows(p):
-        @pl.loop(0, 2 * plan.n_i * (inner // lanes_d))
-        def _(t):
-            chunk = lax.rem(t, inner // lanes_d)
-            which = lax.div(t, inner // lanes_d)
-            i, kk = lax.rem(which, plan.n_i), lax.div(which, plan.n_i)
-            k = jnp.where(kk == 0, 1 - c, c)
+    def partial_copy(t):
+        return remote(psend.at[t], precv.at[t], p_s.at[t], p_r.at[t], partner)
+
+    def step_of(t):
+        return lax.div(t, plan.ph), lax.rem(mp + 1 + lax.rem(t, plan.ph), plan.ph)
+
+    def depth_rows(t):
+        k, p = step_of(t)
+
+        @pl.loop(0, plan.n_i * (inner // lanes_d))
+        def _(u):
+            chunk, i = lax.rem(u, inner // lanes_d), lax.div(u, inner // lanes_d)
             row = i * plan.depth_h + 2 * p + k
             lanes = pl.ds(pl.multiple_of(chunk * lanes_d, lanes_d), lanes_d)
             e = [exp[row + di, :, lanes] for di in range(3)]
@@ -252,56 +272,66 @@
                 + pltpu.roll(sums[2], wide - 1, 0)[:tile_w]
             )
             value = gelu(summed + b_dep[:, lanes]).astype(BF16)
-            dbuf[kk, pl.ds(pl.multiple_of(i * tile_w, tile_w), tile_w), lanes] = value
-
-        psend[p] = dot(dbuf[0], w_proj[...]).astype(BF16)
-        partial_copy(p).start()
-        acc[p] = dot(dbuf[1], w_proj[...])
-
-    def forward_copy(p, q):
+            dbuf[pl.ds(pl.multiple_of(i * tile_w, tile_w), tile_w), lanes] = value
+
+        ordered = dot(perm[...], dbuf[...]).astype(BF16)
+        projected = dot(ordered, w_proj[...])
+        dperm[0] = projected[:part]
+        dperm[1] = projected[part:]
+        psend[t] = dperm[1 - c].astype(BF16)
+        partial_copy(t).start()
+        rows = jnp.concatenate(
+            [cells[i * plan.depth_h + 2 * p + k] for i in range(plan.n_i)], axis=0
+        )
+        placed = dot(perm[pl.ds(pl.multiple_of(c * part, part), part)], rows)
+        acc[t] = dperm[c] + placed + b_proj[...]
+
+    def forward_copy(k, p, q):
         s = p * plan.pw + q
-        return remote(fsend.at[p, q], frecv.at[my_s], f_s.at[s], f_r.at[my_s], peer(s, c))
-
-    def finish(p):
-        partial_copy(p).wait_recv()
-        own = jnp.concatenate(
-            [cells[i * plan.depth_h + 2 * p + c] for i in range(plan.n_i)], axis=0
+        return remote(
+            fsend.at[k, p, q], frecv.at[k, my_s], f_s.at[k, s], f_r.at[k, my_s], peer(s, c)
         )
-        mixed = own.astype(F32) + acc[p] + precv[p].astype(F32) + b_proj[...]
-        moved = dot(perm[...], mixed.astype(BF16)).astype(BF16)
+
+    def finish(t):
+        k, p = step_of(t)
+        partial_copy(t).wait_recv()
+        mixed = (acc[t] + precv[t].astype(F32)).astype(BF16)
         for q in range(plan.pw):
             s = p * plan.pw + q
-            value = moved[q * plan.piece : (q + 1) * plan.piece]
-            fsend[p, q] = value
+            value = mixed[q * plan.piece : (q + 1) * plan.piece]
+            fsend[k, p, q] = value
 
             @pl.when(s == my_s)
             def _():
-                frecv[my_s] = value
+                frecv[k, my_s] = value
 
             @pl.when(s != my_s)
             def _():
-                forward_copy(p, q).start()
-
-    def step_peer(t):
-        return lax.rem(mp + 1 + t, plan.ph)
-
-    depth_rows(step_peer(0))
-
-    @pl.loop(1, plan.ph)
-    def _(t):
-        depth_rows(step_peer(t))
-        finish(step_peer(t - 1))
-
-    finish(step_peer(plan.ph - 1))
+                forward_copy(k, p, q).start()
+
+    loads[2].wait()
+    depth_rows(jnp.int32(0))
+
+    @pl.loop(1, 2 * plan.ph)
+    def _(t):
+        depth_rows(t)
+        finish(t - 1)
+
+    finish(jnp.int32(2 * plan.ph - 1))
+    loads[3].wait()
+    loads[4].wait()
 
     for copy in weights:
         copy.wait_recv()
 
-    @pl.loop(0, plan.sources)
-    def _(s):
-        @pl.when(s != my_s)
-        def _():
-            remote(fsend.at[0, 0], frecv.at[s], f_s.at[s], f_r.at[s], partner).wait_recv()
+    def await_batch(k):
+        @pl.loop(0, plan.sources)
+        def _(s):
+            @pl.when(s != my_s)
+            def _():
+                remote(
+                    fsend.at[0, 0, 0], frecv.at[k, s], f_s.at[k, s], f_r.at[k, s], partner
+                ).wait_recv()
 
     tokens = plan.sources * plan.span
     heads = half // HEAD_DIM
@@ -310,16 +340,18 @@
         ((lane >= h * HEAD_DIM) & (lane < (h + 1) * HEAD_DIM)).astype(F32) for h in range(heads)
     ]
 
-    def return_copy(g, s, side):
+    def return_copy(k, g, s, side):
         rows = pl.ds(g * plan.span, plan.span)
         return remote(
-            osend.at[side, s, rows], oin.at[c, my_s, rows],
-            o_s.at[side, s, g], o_r.at[c, my_s, g], peer(s, side),
+            osend.at[side, k, s, rows], oin.at[mp, k, c, mq, rows],
+            o_s.at[side, k, s, g], o_r.at[c, k, my_s, g], peer(s, side),
         )
 
-    for g in range(plan.groups):
+    for k, g in [(k, g) for k in range(2) for g in range(plan.groups)]:
+        if g == 0:
+            await_batch(k)
         rows = slice(g * plan.span, (g + 1) * plan.span)
-        mixed = frecv[:, rows, :].astype(F32).reshape(tokens, width)
+        mixed = frecv[k, :, rows, :].astype(F32).reshape(tokens, width)
         centered = mixed - jnp.mean(mixed, axis=-1, keepdims=True)
         spread = jnp.mean(centered * centered, axis=-1, keepdims=True)
         normed = (centered * lax.rsqrt(spread + 1e-05) * gain[...]).astype(BF16)
@@ -345,11 +377,11 @@
             lanes = slice(side * half, (side + 1) * half)
             value = (total[:, lanes] + bo_full[side]).astype(BF16)
             value = value.reshape(plan.sources, plan.span, half)
-            osend[side, :, rows, :] = value
+            osend[side, k, :, rows, :] = value
 
             @pl.when(side == c)
             def _():
-                oin[c, my_s, rows] = osend[side, my_s, rows]
+                oin[mp, k, c, mq, rows] = osend[side, k, my_s, rows]
 
         @pl.loop(0, 2 * plan.sources)
         def _(t):
@@ -357,27 +389,26 @@
 
             @pl.when(jnp.logical_not((s == my_s) & (side == c)))
             def _():
-                return_copy(g, s, side).start()
+                return_copy(k, g, s, side).start()
 
     @pl.loop(0, 2 * plan.ph)
     def _(t):
-        p, core = lax.div(t, 2), lax.rem(t, 2)
+        k, p = lax.div(t, plan.ph), lax.rem(t, plan.ph)
         for q in range(plan.pw):
             s = p * plan.pw + q
-
-            @pl.when(jnp.logical_not((s == my_s) & (core == c)))
-            def _():
-                for g in range(plan.groups):
-                    rows = pl.ds(g * plan.span, plan.span)
-                    remote(
-                        osend.at[0, 0, rows], oin.at[core, s, rows],
-                        o_s.at[0, 0, g], o_r.at[core, s, g], partner,
-                    ).wait_recv()
-        arrived = oin[core, pl.ds(p * plan.pw, plan.pw)]
-        arrived = arrived.astype(F32).reshape(plan.slab, half).astype(BF16)
+            for core in range(2):
+                @pl.when(jnp.logical_not((s == my_s) & (core == c)))
+                def _():
+                    for g in range(plan.groups):
+                        rows = pl.ds(g * plan.span, plan.span)
+                        remote(
+                            osend.at[0, 0, 0, rows], oin.at[p, k, core, q, rows],
+                            o_s.at[0, 0, 0, g], o_r.at[core, k, s, g], partner,
+                        ).wait_recv()
+        arrived = oin[p, k].astype(F32).reshape(plan.slab, half).astype(BF16)
         placed = dot(perm_t[...], arrived).astype(BF16)
         for i in range(plan.n_i):
-            out[i * plan.depth_h + 2 * p + core] = placed[i * tile_w : (i + 1) * tile_w]
+            out[i * plan.depth_h + 2 * p + k] = placed[i * tile_w : (i + 1) * tile_w]
 
     @pl.when(has_bot)
     def _():
@@ -398,13 +429,14 @@
     for copy in weights:
         copy.wait_send()
 
-    @pl.loop(0, plan.ph)
-    def _(p):
-        partial_copy(p).wait_send()
+    @pl.loop(0, 2 * plan.ph)
+    def _(t):
+        k, p = step_of(t)
+        partial_copy(t).wait_send()
         for q in range(plan.pw):
             @pl.when(p * plan.pw + q != my_s)
             def _():
-                forward_copy(p, q).wait_send()
+                forward_copy(k, p, q).wait_send()
 
     @pl.loop(0, 2 * plan.sources)
     def _(t):
@@ -412,8 +444,9 @@
 
         @pl.when(jnp.logical_not((s == my_s) & (side == c)))
         def _():
-            for g in range(plan.groups):
-                return_copy(g, s, side).wait_send()
+            for k in range(2):
+                for g in range(plan.groups):
+                    return_copy(k, g, s, side).wait_send()
 
 
 def per_device(
@@ -431,7 +464,7 @@
         edge_own[span_rows + 1 + r, r * tile_w + tile_w - 1] = 1
     perm = plan.permutation()
     args = (
-        cells, w_expand, b_expand[None], w_depth.reshape(9, inner).astype(F32), b_depth[None],
+        cells, w_expand, b_expand[None], w_depth, b_depth[None],
         w_project, b_project[None], ln_gain[None], w_qkv.transpose(1, 0, 2), w_out, b_out[None],
         jnp.asarray(perm, BF16), jnp.asarray(perm.T, BF16),
         jnp.asarray(plan.score_bias()), jnp.asarray(edge_own, BF16),
@@ -442,28 +475,35 @@
     return pl.pallas_call(
         functools.partial(kernel, plan),
         out_shape=jax.ShapeDtypeStruct((tile_h, tile_w, half), BF16),
-        in_specs=[pl.BlockSpec(memory_space=pltpu.VMEM)] * len(args),
+        in_specs=[
+            pl.BlockSpec(memory_space=pl.ANY if at in (0, 1, 5, 8, 9) else pltpu.VMEM)
+            for at in range(len(args))
+        ],
         out_specs=pl.BlockSpec(memory_space=pltpu.VMEM),
         scratch_shapes=[
+            vmem(cells.shape, BF16), vmem(w_expand.shape, BF16), vmem(w_project.shape, BF16),
+            vmem((3, width, half), BF16), vmem((half, width), BF16), vmem((9, inner), F32),
             vmem((tile_h + 2, tile_w + 8, inner), F32),
             vmem((2, tile_w, width), BF16),
             vmem((2, span_rows, width), BF16),
             vmem((2, span_rows, width), BF16),
             vmem((2 * span_rows, inner), F32),
-            vmem((2, n.slab, inner), BF16),
-            vmem((n.ph, n.slab, width), BF16),
-            vmem((n.ph, n.slab, width), BF16),
-            vmem((n.ph, n.slab, width), F32),
-            vmem((n.ph, n.pw, n.piece, width), BF16),
-            vmem((n.sources, n.piece, width), BF16),
+            vmem((n.slab, inner), BF16),
+            vmem((2, n.slab // 2, width), F32),
+            vmem((2 * n.ph, n.slab // 2, width), BF16),
+            vmem((2 * n.ph, n.slab // 2, width), BF16),
+            vmem((2 * n.ph, n.slab // 2, width), F32),
+            vmem((2, n.ph, n.pw, n.piece, width), BF16),
+            vmem((2, n.sources, n.piece, width), BF16),
             vmem((3, width, half), BF16),
             vmem((half, width), BF16),
             vmem((2, 1, half), F32),
-            vmem((2, n.sources, n.piece, half), BF16),
-            vmem((2, n.sources, n.piece, half), BF16),
+            vmem((2, 2, n.sources, n.piece, half), BF16),
+            vmem((n.ph, 2, 2, n.pw, n.piece, half), BF16),
+            dma((5,)),
             dma((2,)), dma((2,)), dma((2,)), dma((2,)), dma((3,)), dma((3,)),
-            dma((n.ph,)), dma((n.ph,)), dma((n.sources,)), dma((n.sources,)),
-            dma((2, n.sources, n.groups)), dma((2, n.sources, n.groups)),
+            dma((2 * n.ph,)), dma((2 * n.ph,)), dma((2, n.sources)), dma((2, n.sources)),
+            dma((2, 2, n.sources, n.groups)), dma((2, 2, n.sources, n.groups)),
         ],
         compiler_params=pltpu.CompilerParams(
             collective_id=0, has_side_effects=True, vmem_limit_bytes=60 << 20

time: 55.9 us -> 47.8 us (0.86)
  Pallas kernels: 52.4 us -> 45.7 us
  local copies, waits for them, and re-layouts: 3.26 us -> 1.88 us
    pallas_call x1, Pallas kernels: 52.4 us -> 45.7 us  [per_device(): pl.pallas_call(functools.partial(kernel, plan), out_shape=jax.ShapeDtypeS...]
    convert_element_type x1 -> x0, local copies, waits for them, and re-layouts: 1.38 us -> none  [per_device(): w_depth.reshape(9, inner).astype(F32)]
where the time goes in v2:
time: 47.8 us; the launch traced here: 47.6 us
  Pallas kernels  45.7 us (96%)
  local copies, waits for them, and re-layouts  1.88 us (4%)
    pallas_call x1, Pallas kernels, per_device(): pl.pallas_call(functools.partial(kernel, plan), out_shape=jax.ShapeDtypeS...  45.7 us
    unnamed x1, local copies, waits for them, and re-layouts  1.88 us

profile of v2, /device:TPU:0, one launch (start us, length us, event | category | flops | bytes accessed | tf_op | source)
XLA Modules:
  0.0 47.6 jit_solution(3464730572364827004)
XLA Ops:
  0.0 45.7 %shard_map.145 = bf16[16,64,256]{2,1,0:T(8,128)(2,1)} custom-call(bf16[16,64,512]{2,1,0:T(8,128)(2,1)} %cells_h.1, bf16[512,1024]{1,0:T(8,128)(2,1)} %w_exp_h.1, f32[1,1024]{1,0:T(1,128)} %bitcast.7, bf16[3,3,1024]{2,1,0:T(4,128)(2,1)} %w_dep_in.1, f32[1,1024]{1,0:T(1,128)} %bitcast.8, bf16[1024,512]{1,0:T(8,128)(2,1)} %w_proj_h.1, f32[1,512]{1,0:T(1,128)} %bitcast.9, ...), custom_call_target="tpu_custom_call" | custom-call | tf_op jit(solution)/shard_map/pallas_call | solution.py:475
  45.7 1.9 %copy.17 = bf16[16,64,256]{2,1,0:T(8,128)(2,1)} copy(bf16[16,64,256]{2,1,0:T(8,128)(2,1)} %shard_map.145) | data formatting | bytes 1048576
